TPU v7x, 128 devices: a whole 4x4x4 slice. The times are simulated.
128 devices in a mesh: cuts: 2 (over x_hi), section: 4 (over y), dp: 16 (over z, x_lo, core).
Axes of the slice: x: 4 (x_hi: 2, x_lo: 2; x = x_hi * 2 + x_lo), y: 4, z: 4, core: 2. Of those that a mesh axis runs over, the one named last changes fastest.
Arguments:
- activations: bfloat16 [2, 4, 4096, 4096], P('cuts', 'section', 'dp'), may hold values from -6 to 6
- upstream_grad: bfloat16 [2, 4, 4096, 4096], P('cuts', 'section', 'dp'), may hold values from -6 to 6
- routes: int32 [2, 4, 4096, 4], P('cuts', 'section', 'dp'), may hold values from 0 to 15, as said below
- router_probs: float32 [2, 4, 4096, 4], P('cuts', 'section', 'dp'), may hold values from 0.2 to 1
- gate_weight: bfloat16 [4, 5376, 4096], P('section', 'dp'), may hold values from -0.09375 to 0.09375
- up_weight: bfloat16 [4, 5376, 4096], P('section', 'dp'), may hold values from -0.09375 to 0.09375
- down_weight: bfloat16 [4, 5376, 4096], P('section', 'dp'), may hold values from -0.078125 to 0.078125
Outputs:
- grad_gate: bfloat16 [4, 5376, 4096], P('section', 'dp')
- grad_up: bfloat16 [4, 5376, 4096], P('section', 'dp')
- grad_down: bfloat16 [4, 5376, 4096], P('section', 'dp')
- prev_grad: bfloat16 [2, 4, 4096, 4096], P('cuts', 'section', 'dp')
Inputs may be any that keep to these rules, and one draw needn't show every extreme that they name: `routes`: each token names 4 different experts. In every aligned block of 256 tokens of one replica and section, from 32 to 64 tokens name expert 0, and in every draw some block has exactly 64.
All inputs are finite; a program needn't handle non-finite values.
Results may differ from a plain program's by a relative error of at most 0.025.
Values may be sent and summed in bfloat16 or wider, within the bound.
No kernel may reach another device: no remote copies, remote signals or barrier semaphores. Data moves between devices by JAX's collectives and lax.ppermute only.
A program may use at most 192 MiB of HBM per device.

v0:
```python
import jax
import jax.numpy as jnp
from jax import lax
from jax.sharding import PartitionSpec as P

CAP = 64


def from_behind(block, axis, distance):
    devices = range(lax.axis_size(axis))
    route = [(i - distance, i) for i in devices if i - distance in devices]
    return lax.ppermute(block, axis, route)


def contract_last(left, right):
    return lax.dot_general(
        left, right, (((1,), (1,)), ((), ())), preferred_element_type=jnp.float32
    )


def contract_first(left, right):
    return lax.dot_general(
        left, right, (((0,), (0,)), ((), ())), preferred_element_type=jnp.float32
    )


def per_device(
    activations, upstream_grad, routes, router_probs, gate_weight, up_weight, down_weight
):
    local_acts = activations[0, 0]
    local_grads = upstream_grad[0, 0]
    expert_hits = routes[0, 0] == 0
    router_weight = jnp.sum(jnp.where(expert_hits, router_probs[0, 0], jnp.float32(0.0)), axis=1)
    is_routed = jnp.any(expert_hits, axis=1)
    row_index = jnp.cumsum(is_routed.astype(jnp.int32)) - 1
    wanted = jnp.arange(CAP, dtype=jnp.int32)
    picker = ((row_index[None, :] == wanted[:, None]) & is_routed[None, :]).astype(jnp.bfloat16)
    scaled = (router_weight[:, None] * local_grads.astype(jnp.float32)).astype(jnp.bfloat16)
    packed_acts = jnp.dot(picker, local_acts, preferred_element_type=jnp.float32).astype(
        jnp.bfloat16
    )
    packed_grads = jnp.dot(picker, scaled, preferred_element_type=jnp.float32).astype(jnp.bfloat16)
    rows_acts, rows_grads = (
        lax.all_gather(packed_acts, "dp", axis=0, tiled=True),
        lax.all_gather(packed_grads, "dp", axis=0, tiled=True),
    )
    gate_local = gate_weight[0]
    up_local = up_weight[0]
    down_local = down_weight[0]
    gate_pre = contract_last(rows_acts, gate_local)
    up_pre = contract_last(rows_acts, up_local)
    sig_gate = jax.nn.sigmoid(gate_pre)
    silu_gate = gate_pre * sig_gate
    hidden = (silu_gate * up_pre).astype(jnp.bfloat16)
    hidden_grad = contract_last(rows_grads, down_local)
    gate_grad = (hidden_grad * up_pre * sig_gate * (1.0 + gate_pre * (1.0 - sig_gate))).astype(
        jnp.bfloat16
    )
    up_grad = (hidden_grad * silu_gate).astype(jnp.bfloat16)
    down_part = contract_first(hidden, rows_grads)
    gate_part = contract_first(gate_grad, rows_acts)
    up_part = contract_first(up_grad, rows_acts)
    gate_total, up_total, down_total = (
        lax.psum(gate_part.astype(jnp.bfloat16), "cuts").astype(jnp.float32),
        lax.psum(up_part.astype(jnp.bfloat16), "cuts").astype(jnp.float32),
        lax.psum(down_part.astype(jnp.bfloat16), "cuts").astype(jnp.float32),
    )
    input_rows = lax.psum_scatter(
        (
            jnp.dot(gate_grad, gate_local, preferred_element_type=jnp.float32)
            + jnp.dot(up_grad, up_local, preferred_element_type=jnp.float32)
        ).astype(jnp.bfloat16),
        "dp",
        scatter_dimension=0,
        tiled=True,
    )
    token_grad = contract_first(picker, input_rows).astype(jnp.bfloat16)
    prev_grad = from_behind(token_grad[None, None], "section", -1)
    grad_gate = gate_total.astype(jnp.bfloat16)[None]
    grad_up = up_total.astype(jnp.bfloat16)[None]
    grad_down = down_total.astype(jnp.bfloat16)[None]
    return (grad_gate, grad_up, grad_down, prev_grad)


def solution(mesh):
    placed = (
        P("cuts", "section", "dp", None),
        P("cuts", "section", "dp", None),
        P("cuts", "section", "dp", None),
        P("cuts", "section", "dp", None),
        P("section", "dp", None),
        P("section", "dp", None),
        P("section", "dp", None),
    )
    return jax.shard_map(
        per_device,
        mesh=mesh,
        in_specs=placed,
        out_specs=(
            P("section", "dp", None),
            P("section", "dp", None),
            P("section", "dp", None),
            P("cuts", "section", "dp", None),
        ),
        check_vma=False,
    )
```

profile of v0, /device:TPU:12, one launch (start us, length us, event | category | flops | bytes accessed | tf_op | source)
XLA Modules:
  0.0 468.4 jit_solution(16867495214857487981)
XLA Ops:
  7.2 0.0 copy-start
  7.2 0.0 all-gather.5.cloned.1.call-start
  7.2 0.9 select_reduce_fusion
  8.1 0.3 reduce-window.9
  8.4 0.1 slice.7
  8.6 0.1 slice_reduce_fusion
  8.7 0.1 add_bitcast_fusion
  8.7 2.9 convolution_convert_fusion.4
  11.6 0.0 all-gather.5.cloned.1.call-update
  11.6 0.0 all-gather.3.cloned.1.call-start
  11.7 3.0 convolution_convert_fusion.5
  14.7 0.0 all-gather.3.cloned.1.call-update
  14.7 0.0 reduce-scatter.2.cloned.1.call-start
  14.8 51.4 %all-gather.5.cloned.1.call-done = bf16[1024,4096]{1,0:T(8,128)(2,1)} async-done(((bf16[64,4096]{1,0:T(8,128)(2,1)}), bf16[1024,4096]{1,0:T(8,128)(2,1)}) %all-gather.5.cloned.1.call-update) | async-done | bytes 8388624 | tf_op jit(solution)/shard_map/all_gather | solution.py:44
  66.2 0.0 copy-done
  66.2 0.0 copy-start.4
  66.2 0.0 copy-start.10
  66.2 7.6 %fusion.7 = f32[1024,336]{0,1:T(8,128)} fusion(bf16[1024,4096]{1,0:T(8,128)(2,1)} %all-gather.5.cloned.1.call-done, bf16[1,336,4096]{2,1,0:T(8,128)(2,1)S(1)} %copy-done), kind=kOutput, calls=%fused_computation.15 | convolution fusion | flops 2818572288 | bytes 12517376 | tf_op jit(solution)/shard_map/dot_general | solution.py:16
  73.8 0.0 copy-done.4
  73.8 0.0 copy-done.10
  73.9 4.1 fusion.10
  78.0 43.7 %all-gather.3.cloned.1.call-done = bf16[1024,4096]{1,0:T(8,128)(2,1)} async-done(((bf16[64,4096]{1,0:T(8,128)(2,1)}), bf16[1024,4096]{1,0:T(8,128)(2,1)}) %all-gather.3.cloned.1.call-update) | async-done | bytes 8388624 | tf_op jit(solution)/shard_map/all_gather | solution.py:45
  121.6 8.3 %multiply_convert_fusion.1 = (bf16[1024,336]{0,1:T(8,128)(2,1)S(1)}, bf16[1024,336]{0,1:T(8,128)(2,1)S(1)}) fusion(f32[1024,336]{0,1:T(8,128)} %fusion.7, f32[1024,336]{0,1:T(8,128)} %fusion.10, bf16[1024,4096]{1,0:T(8,128)(2,1)} %all-gather.3.cloned.1.call-done, bf16[1,336,4096]{2,1,0:T(8,128)(2,1)} %param.13), kind=kOutput, calls=%fused_computation.26 | convolution fusion | flops 2823045120 | bytes 15269888 | tf_op jit(solution)/shard_map/dot_general | solution.py:16
  130.0 0.0 copy-start.8
  130.0 0.0 copy-start.5
  130.0 8.3 %fusion.5 = f32[1024,4096]{1,0:T(8,128)} fusion(bf16[1024,336]{0,1:T(8,128)(2,1)S(1)} %get-tuple-element.10, bf16[1,336,4096]{2,1,0:T(8,128)(2,1)S(1)} %copy-done), kind=kOutput, calls=%fused_computation.13 | convolution fusion | flops 2818572288 | bytes 20217856 | tf_op jit(solution)/shard_map/dot_general | solution.py:70
  138.3 0.0 copy-done.8
  138.3 0.0 copy-done.5
  138.3 10.2 %add_convert_fusion = bf16[1024,4096]{1,0:T(8,128)(2,1)} fusion(f32[1024,4096]{1,0:T(8,128)} %fusion.5, bf16[1024,336]{0,1:T(8,128)(2,1)S(1)} %get-tuple-element.9, bf16[1,336,4096]{2,1,0:T(8,128)(2,1)S(1)} %copy-done.5), kind=kOutput, calls=%fused_computation | convolution fusion | flops 2826960896 | bytes 28606464 | tf_op jit(solution)/shard_map/dot_general | solution.py:71
  148.5 0.0 reduce-scatter.2.cloned.1.call-update
  148.5 0.0 copy-start.9
  148.5 0.0 all-reduce.3.cloned.1.call-start
  148.6 0.0 slice-start
  148.6 7.8 %fusion.1 = bf16[1,336,4096]{2,1,0:T(8,128)(2,1)} fusion(bf16[1024,336]{0,1:T(8,128)(2,1)S(1)} %get-tuple-element.9, bf16[1024,4096]{1,0:T(8,128)(2,1)} %all-gather.5.cloned.1.call-done), kind=kOutput, calls=%fused_computation.6 | convolution fusion | flops 2819948544 | bytes 11829248 | tf_op jit(solution)/shard_map/dot_general | solution.py:22
  156.4 0.0 copy-done.9
  156.4 0.0 slice-start.1
  156.4 0.0 copy-start.11
  156.4 0.0 copy-start.12
  156.4 8.2 %fusion = bf16[1,336,4096]{2,1,0:T(8,128)(2,1)} fusion(bf16[1024,336]{0,1:T(8,128)(2,1)S(1)} %copy-done.9, bf16[1024,4096]{1,0:T(8,128)(2,1)} %all-gather.5.cloned.1.call-done), kind=kOutput, calls=%fused_computation.5 | convolution fusion | flops 2819948544 | bytes 11829248 | tf_op jit(solution)/shard_map/dot_general | solution.py:22
  164.7 0.0 slice-done
  164.7 0.0 slice-done.1
  164.7 0.0 copy-done.11
  164.7 0.0 copy-done.12
  164.7 4.5 fusion.2
  169.2 0.0 all-reduce.3.cloned.1.call-update
  169.3 78.1 %reduce-scatter.2.cloned.1.call-done = bf16[64,4096]{1,0:T(8,128)(2,1)} async-done(((bf16[1024,4096]{1,0:T(8,128)(2,1)}), bf16[64,4096]{1,0:T(8,128)(2,1)}) %reduce-scatter.2.cloned.1.call-update) | async-done | bytes 524304 | tf_op jit(solution)/shard_map/reduce_scatter | solution.py:68
  247.3 1.8 fusion.3
  249.1 2.5 collective-permute-start
  251.6 44.9 %collective-permute-done = bf16[1,1,256,4096]{3,2,1,0:T(8,128)(2,1)S(1)} collective-permute-done((bf16[1,1,256,4096]{3,2,1,0:T(8,128)(2,1)S(1)}, bf16[1,1,256,4096]{3,2,1,0:T(8,128)(2,1)S(1)}, u32[]{:S(2)}, u32[]{:S(2)}) %collective-permute-start) | collective-permute-done | bytes 2097184 | tf_op jit(solution)/shard_map/ppermute | solution.py:12
  296.5 0.0 copy-start.6
  296.5 154.9 %all-reduce.3.cloned.1.call-done = (bf16[1,336,4096]{2,1,0:T(8,128)(2,1)}, bf16[1,336,4096]{2,1,0:T(8,128)(2,1)}, bf16[1,336,4096]{2,1,0:T(8,128)(2,1)}) async-done(((bf16[1,336,4096]{2,1,0:T(8,128)(2,1)}, bf16[1,336,4096]{2,1,0:T(8,128)(2,1)}, bf16[1,336,4096]{2,1,0:T(8,128)(2,1)}), (bf16[1,336,4096]{2,1,0:T(8,128)(2,1)}, bf16[1,336,4096]{2,1,0:T(8,128)(2,1)}, ...) | async-done | bytes 8257552 | tf_op jit(solution)/shard_map/psum | solution.py:64
  451.4 0.0 copy-done.6
  451.4 0.0 copy-start.3
  451.4 3.8 copy.15
  455.2 0.0 copy-done.3
  455.2 0.0 copy-start.2
  455.2 1.5 copy.16
  456.7 1.2 copy-done.2
  458.0 0.0 copy-start.7
  458.0 0.0 copy-start.1
  458.0 1.5 copy.17
  459.5 1.0 copy-done.7
  460.5 1.3 copy.18
  461.9 0.0 copy-done.1
  (4 shorter events, 0.1 us)
Async XLA Ops:
  7.2 59.0 %copy-start = (bf16[1,336,4096]{2,1,0:T(8,128)(2,1)S(1)}, bf16[1,336,4096]{2,1,0:T(8,128)(2,1)}, u32[]{:S(2)}) copy-start(bf16[1,336,4096]{2,1,0:T(8,128)(2,1)} %param.11) | copy-start | bytes 8257540
  7.2 59.0 %all-gather.5.cloned.1.call-start = ((), (), s32[]{:S(2)}) async-start(), calls=%async_computation.2 | async-start | bytes 8912896 | tf_op jit(solution)/shard_map/all_gather | solution.py:44
  11.6 110.0 %all-gather.3.cloned.1.call-start = ((), (), s32[]{:S(2)}) async-start(), calls=%async_computation.1 | async-start | bytes 8912896 | tf_op jit(solution)/shard_map/all_gather | solution.py:45
  14.7 232.6 %reduce-scatter.2.cloned.1.call-start = ((), (), s32[]{:S(2)}) async-start(), calls=%async_computation.3 | async-start | bytes 8912896 | tf_op jit(solution)/shard_map/reduce_scatter | solution.py:68
  66.2 7.6 %copy-start.4 = (bf16[1,336,4096]{2,1,0:T(8,128)(2,1)S(1)}, bf16[1,336,4096]{2,1,0:T(8,128)(2,1)}, u32[]{:S(2)}) copy-start(bf16[1,336,4096]{2,1,0:T(8,128)(2,1)} %param.12) | copy-start | bytes 8257540
  66.2 7.6 %copy-start.10 = (bf16[1024,4096]{1,0:T(8,128)(2,1)S(1)}, bf16[1024,4096]{1,0:T(8,128)(2,1)}, u32[]{:S(2)}) copy-start(bf16[1024,4096]{1,0:T(8,128)(2,1)} %all-gather.5.cloned.1.call-done) | copy-start | bytes 25165828
  130.0 8.3 %copy-start.8 = (bf16[1024,336]{0,1:T(8,128)(2,1)}, bf16[1024,336]{0,1:T(8,128)(2,1)S(1)}, u32[]{:S(2)}) copy-start(bf16[1024,336]{0,1:T(8,128)(2,1)S(1)} %get-tuple-element.10) | copy-start | bytes 2064388
  130.0 8.3 %copy-start.5 = (bf16[1,336,4096]{2,1,0:T(8,128)(2,1)S(1)}, bf16[1,336,4096]{2,1,0:T(8,128)(2,1)}, u32[]{:S(2)}) copy-start(bf16[1,336,4096]{2,1,0:T(8,128)(2,1)} %param.12) | copy-start | bytes 8257540
  148.5 7.9 %copy-start.9 = (bf16[1024,336]{0,1:T(8,128)(2,1)S(1)}, bf16[1024,336]{0,1:T(8,128)(2,1)}, u32[]{:S(2)}) copy-start(bf16[1024,336]{0,1:T(8,128)(2,1)} %copy-done.8) | copy-start | bytes 2064388
  148.5 302.9 %all-reduce.3.cloned.1.call-start = ((), (), s32[]{:S(2)}) async-start(), calls=%async_computation.4 | async-start | bytes 16515072 | tf_op jit(solution)/shard_map/psum | solution.py:64
  148.6 16.1 %slice-start = ((s8[8388608]{0:T(1024)(128)(4,1)}), s8[4194304]{0:T(1024)(128)(4,1)S(1)}, s32[]{:S(2)}) async-start(s8[8388608]{0:T(1024)(128)(4,1)} %bitcast.47), calls=%async_computation.5 | async-start | bytes 8388608
  156.4 8.3 %slice-start.1 = ((s8[8388608]{0:T(1024)(128)(4,1)}), s8[4194304]{0:T(1024)(128)(4,1)S(1)}, s32[]{:S(2)}) async-start(s8[8388608]{0:T(1024)(128)(4,1)} %bitcast.47), calls=%async_computation.6 | async-start | bytes 8388608
  156.4 8.3 %copy-start.11 = (f32[1024,336]{0,1:T(8,128)S(1)}, f32[1024,336]{0,1:T(8,128)}, u32[]{:S(2)}) copy-start(f32[1024,336]{0,1:T(8,128)} %fusion.7) | copy-start | bytes 4128772
  156.4 8.3 %copy-start.12 = (f32[1024,336]{0,1:T(8,128)S(1)}, f32[1024,336]{0,1:T(8,128)}, u32[]{:S(2)}) copy-start(f32[1024,336]{0,1:T(8,128)} %fusion.10) | copy-start | bytes 4128772
  249.1 47.4 %collective-permute-start = (bf16[1,1,256,4096]{3,2,1,0:T(8,128)(2,1)S(1)}, bf16[1,1,256,4096]{3,2,1,0:T(8,128)(2,1)S(1)}, u32[]{:S(2)}, u32[]{:S(2)}) collective-permute-start(bf16[1,1,256,4096]{3,2,1,0:T(8,128)(2,1)S(1)} %fusion.3), channel_id=1, source_target_pairs={{16,0},{32,16},{48,32},{17,1},{33,17},{49,33},{18,2},{34,18},{50,3... | collective-permute-start | bytes 6291464 | tf_op jit(solution)/shard_map/ppermute | solution.py:12
  296.5 154.9 %copy-start.6 = (bf16[1,1,256,4096]{3,2,1,0:T(8,128)(2,1)}, bf16[1,1,256,4096]{3,2,1,0:T(8,128)(2,1)S(1)}, u32[]{:S(2)}) copy-start(bf16[1,1,256,4096]{3,2,1,0:T(8,128)(2,1)S(1)} %collective-permute-done) | copy-start | bytes 6291460
  451.4 3.8 copy-start.3
  455.2 2.8 copy-start.2
  458.0 2.6 copy-start.7
  458.0 3.9 copy-start.1
Sparse Core Ops, SparseCore 0:
  11.8 54.3 all-gather.4
  68.5 53.1 all-gather.2
  148.6 98.6 reduce-scatter.1
  250.6 200.7 all-reduce.2
where the time goes:
time: 472 us; the launch traced here: 468 us
  waiting for transfers between devices  373 us (79%)
  matrix products  66.8 us (14%)
  between operations  13.9 us (3%)
  local copies, waits for them, and re-layouts  10.7 us (2%)
    psum x1, waiting for transfers between devices, per_device(): lax.psum(gate_part.astype(jnp.bfloat16), 'cuts').astype(jnp.float32)  155 us
    reduce_scatter x1, waiting for transfers between devices, per_device(): lax.psum_scatter((jnp.dot(gate_grad, gate_local, preferred_element_type=j...  78.1 us
    all_gather x1, waiting for transfers between devices, per_device(): lax.all_gather(packed_acts, 'dp', axis=0, tiled=True)  51.4 us
    ppermute x1, waiting for transfers between devices, from_behind(): return lax.ppermute(block, axis, route)  44.9 us
    all_gather x1, waiting for transfers between devices, per_device(): lax.all_gather(packed_grads, 'dp', axis=0, tiled=True)  43.7 us
    dot_general x4, matrix products, contract_first(): lax.dot_general(left, right, (((0,), (0,)), ((), ())), preferred_element_...  22.4 us
    dot_general x3, matrix products, contract_last(): lax.dot_general(left, right, (((1,), (1,)), ((), ())), preferred_element_...  20.1 us
    unnamed x34, local copies, waits for them, and re-layouts  10.5 us
  transfers between devices with their start and end apart: 5, of which 5 were waited for; matrix products, arithmetic and copies ran while one was open for 8% of the time, Pallas kernels for 0%

commit v1 on v0

v1 whole, which is shorter than its diff:
```python
import jax
import jax.numpy as jnp
from jax import lax
from jax.sharding import PartitionSpec as P

CAP = 64
AXES = ("cuts", "dp")


def place(x, z, core):
    return (x // 2) * 16 + z * 4 + (x % 2) * 2 + core


def route(fx, fz, fc):
    return [
        (place(x, z, c), place(fx(x) % 4, fz(z) % 4, fc(c)))
        for x in range(4)
        for z in range(4)
        for c in range(2)
    ]


def keep(v):
    return v


INNER = route(lambda x: x ^ 1, keep, keep)
OUTER = route(lambda x: 3 - x, keep, keep)
UP = route(keep, lambda z: z + 1, keep)
DOWN = route(keep, lambda z: z - 1, keep)
ACROSS = route(keep, lambda z: z + 2, keep)
SIBLING = route(keep, keep, lambda c: 1 - c)


def send(value, pairs):
    return lax.ppermute(value, AXES, pairs)


def join(*parts):
    return jnp.concatenate(parts, axis=0)


def x_ring(v):
    h = v.shape[0] // 2
    inner, outer = send(v, INNER), send(v, OUTER)
    return inner, outer, send(outer[:h], INNER), send(inner[h:], OUTER)


def z_ring(v):
    h = v.shape[0] // 2
    below, above = send(v, UP), send(v, DOWN)
    return below, above, send(below[:h], UP), send(above[h:], DOWN)


def contract_last(left, right):
    return lax.dot_general(
        left, right, (((1,), (1,)), ((), ())), preferred_element_type=jnp.float32
    )


def contract_first(left, right):
    return lax.dot_general(
        left, right, (((0,), (0,)), ((), ())), preferred_element_type=jnp.float32
    )


def matmul(left, right):
    return jnp.dot(left, right, preferred_element_type=jnp.float32)


def half(v):
    return v.astype(jnp.bfloat16)


def full(v):
    return v.astype(jnp.float32)


def per_device(
    activations, upstream_grad, routes, router_probs, gate_weight, up_weight, down_weight
):
    local_acts = activations[0, 0]
    local_grads = upstream_grad[0, 0]
    expert_hits = routes[0, 0] == 0
    router_weight = jnp.sum(jnp.where(expert_hits, router_probs[0, 0], jnp.float32(0.0)), axis=1)
    is_routed = jnp.any(expert_hits, axis=1)
    before = jnp.arange(256)[None, :] <= jnp.arange(256)[:, None]
    count = jnp.sum(jnp.where(before & is_routed[None, :], 1, 0), axis=1)
    slot = jnp.where(is_routed, count, 0)
    wanted = jnp.arange(1, CAP + 1, dtype=jnp.int32)
    picker = half(slot[None, :] == wanted[:, None])
    scaled = half(router_weight[:, None] * full(local_grads))
    acts = half(matmul(picker, local_acts))
    grads = half(matmul(picker, scaled))
    next_slot = lax.ppermute(slot, "section", [(1, 0), (2, 1), (3, 2)])
    gate_local, up_local, down_local = gate_weight[0], up_weight[0], down_weight[0]

    acts_x = join(acts, *x_ring(acts))
    grads_z = join(grads, *z_ring(grads))
    near, far = acts_x[:128], acts_x[128:]
    near_z = z_ring(near)
    far_z = z_ring(far)
    grads_x = x_ring(grads_z)
    def column(base, ring, k):
        across = join(ring[2], ring[3])
        return join(*[v[k * 64 : k * 64 + 64] for v in (base, ring[0], ring[1], across)])

    acts_of = [column(near, near_z, 0), column(near, near_z, 1), column(far, far_z, 0), column(far, far_z, 1)]
    grads_of = [grads_z, grads_x[0], grads_x[1], join(grads_x[2], grads_x[3])]

    def forward(rows_acts, rows_grads):
        gate_pre = contract_last(rows_acts, gate_local)
        up_pre = contract_last(rows_acts, up_local)
        sig_gate = jax.nn.sigmoid(gate_pre)
        silu_gate = gate_pre * sig_gate
        hidden_grad = contract_last(rows_grads, down_local)
        hidden = half(silu_gate * up_pre)
        gate_grad = half(hidden_grad * up_pre * sig_gate * (1.0 + gate_pre * (1.0 - sig_gate)))
        up_grad = half(hidden_grad * silu_gate)
        return hidden, gate_grad, up_grad

    all_acts, all_grads, outs = [], [], []
    for k in range(4):
        mine = join(acts_of[k], grads_of[k])
        theirs = send(mine, SIBLING)
        rows_a = join(mine[:256], theirs[:256])
        rows_g = join(mine[256:], theirs[256:])
        all_acts.append(rows_a)
        all_grads.append(rows_g)
        outs.append(forward(rows_a, rows_g))

    terms = [half(matmul(outs[k][1], gate_local) + matmul(outs[k][2], up_local)) for k in range(2)]
    from_core = send(join(terms[0][256:], terms[1][256:]), SIBLING)
    own = half(full(terms[0][:256]) + full(from_core[:256]))
    inner = half(full(terms[1][:256]) + full(from_core[256:]))
    own_l, inner_l, own_r, inner_r = own[:, :2048], inner[:, :2048], own[:, 2048:], inner[:, 2048:]
    both_r = join(own_r.reshape(4, 64, 2048), inner_r.reshape(4, 64, 2048)).reshape(2, 4, 64, 2048)
    left = full(own_l) + full(send(inner_l, INNER))
    z_r = [
        full(both_r[:, 0]),
        full(send(both_r[:, 1], DOWN)),
        full(send(both_r[:, 2], UP)),
        full(send(both_r[:, 3], ACROSS)),
    ]
    right2 = (z_r[0] + z_r[1]) + (z_r[2] + z_r[3])
    right = right2[0] + full(send(half(right2[1]), INNER))
    left_b = half(left)
    left = (left[:64] + full(send(left_b[64:128], DOWN))) + (
        full(send(left_b[128:192], UP)) + full(send(left_b[192:], ACROSS))
    )
    input_rows = jnp.concatenate([half(left), half(right)], axis=1)
    shifted = lax.ppermute(input_rows, "section", [(1, 0), (2, 1), (3, 2)])
    placer = half(next_slot[:, None] == wanted[None, :])
    prev_grad = half(matmul(placer, shifted))[None, None]

    rows_acts, rows_grads = join(*all_acts), join(*all_grads)
    hidden, gate_grad, up_grad = (join(*[o[i] for o in outs]) for i in range(3))
    grad_down = half(contract_first(hidden, rows_grads))[None]
    grad_gate = half(contract_first(gate_grad, rows_acts))[None]
    grad_up = half(contract_first(up_grad, rows_acts))[None]
    return (grad_gate, grad_up, grad_down, prev_grad)


def solution(mesh):
    placed = (
        P("cuts", "section", "dp", None),
        P("cuts", "section", "dp", None),
        P("cuts", "section", "dp", None),
        P("cuts", "section", "dp", None),
        P("section", "dp", None),
        P("section", "dp", None),
        P("section", "dp", None),
    )
    return jax.shard_map(
        per_device,
        mesh=mesh,
        in_specs=placed,
        out_specs=(
            P("section", "dp", None),
            P("section", "dp", None),
            P("section", "dp", None),
            P("cuts", "section", "dp", None),
        ),
        check_vma=False,
    )
```

time: 472 us -> 358 us (0.76)
  waiting for transfers between devices: 373 us -> 168 us
  local copies, waits for them, and re-layouts: 10.7 us -> 62.5 us
  starting transfers between devices: 2.62 us -> 38.5 us
  between operations: 13.9 us -> 1.51 us
  matrix products: 66.8 us -> 75.2 us
  other arithmetic: 1.32 us -> 6.15 us
    psum x1 -> x0, waiting for transfers between devices: 155 us -> none  [per_device(): lax.psum(gate_part.astype(jnp.bfloat16), 'cuts').astype(jnp.float32)]
    ppermute x1 -> x35, waiting for transfers between devices: 44.9 us -> 168 us  [the longest x33 164 us: send(): return lax.ppermute(value, AXES, pairs)]
    all_gather x2 -> x0, waiting for transfers between devices: 95.1 us -> none  [the longest x1 51.4 us: per_device(): lax.all_gather(packed_acts, 'dp', axis=0, tiled=True)]
    reduce_scatter x1 -> x0, waiting for transfers between devices: 78.1 us -> none  [per_device(): lax.psum_scatter((jnp.dot(gate_grad, gate_local, preferred_element_type=j...]
    unnamed x34 -> x108, local copies, waits for them, and re-layouts: 10.5 us -> 55.4 us
    ppermute x1 -> x35, starting transfers between devices: 2.46 us -> 38.5 us  [the longest x33 33.8 us: send(): return lax.ppermute(value, AXES, pairs)]
    dot_general x4 -> x3, matrix products: 22.4 us -> 33.5 us  [contract_first(): lax.dot_general(left, right, (((0,), (0,)), ((), ())), preferred_element_...]
    dot_general x4 -> x7, matrix products: 24.4 us -> 16.2 us  [matmul(): return jnp.dot(left, right, preferred_element_type=jnp.float32)]
  transfers between devices with their start and end apart: 5 -> 35, of which waited for: 5 -> 19; matrix products, arithmetic and copies ran while one was open for 8% -> 24% of each run, Pallas kernels for 0% -> 0%
where the time goes in v1:
time: 358 us; the launch traced here: 351 us
  waiting for transfers between devices  168 us (47%)
  matrix products  75.2 us (21%)
  local copies, waits for them, and re-layouts  62.5 us (17%)
  starting transfers between devices  38.5 us (11%)
  other arithmetic  6.15 us (2%)
    ppermute x33, waiting for transfers between devices, send(): return lax.ppermute(value, AXES, pairs)  164 us
    unnamed x108, local copies, waits for them, and re-layouts  55.4 us
    ppermute x33, starting transfers between devices, send(): return lax.ppermute(value, AXES, pairs)  33.8 us
    dot_general x3, matrix products, contract_first(): lax.dot_general(left, right, (((0,), (0,)), ((), ())), preferred_element_...  33.5 us
    dot_general x12, matrix products, contract_last(): lax.dot_general(left, right, (((1,), (1,)), ((), ())), preferred_element_...  25.6 us
    dot_general x7, matrix products, matmul(): return jnp.dot(left, right, preferred_element_type=jnp.float32)  16.2 us
  transfers between devices with their start and end apart: 35, of which 19 were waited for; matrix products, arithmetic and copies ran while one was open for 24% of the time, Pallas kernels for 0%

profile of v1, /device:TPU:12, one launch (start us, length us, event | category | flops | bytes accessed | tf_op | source)
XLA Modules:
  0.0 351.5 jit_solution(5221459830876286902)
XLA Ops:
  1.7 2.9 constant_dynamic-update-slice_fusion.7
  5.8 12.5 %collective-permute-done.4 = bf16[64,4096]{1,0:T(8,128)(2,1)S(1)} collective-permute-done((bf16[64,4096]{1,0:T(8,128)(2,1)S(1)}, bf16[64,4096]{1,0:T(8,128)(2,1)S(1)}, u32[]{:S(2)}, u32[]{:S(2)}) %collective-permute-start.4) | collective-permute-done | bytes 524320 | tf_op jit(solution)/shard_map/ppermute | solution.py:36
  18.4 2.0 collective-permute-start.5
  20.4 2.2 collective-permute-start.6
  22.6 22.2 %collective-permute-done.5 = bf16[128,4096]{1,0:T(8,128)(2,1)S(1)} collective-permute-done((bf16[128,4096]{1,0:T(8,128)(2,1)S(1)}, bf16[128,4096]{1,0:T(8,128)(2,1)S(1)}, u32[]{:S(2)}, u32[]{:S(2)}) %collective-permute-start.5) | collective-permute-done | bytes 1048608 | tf_op jit(solution)/shard_map/ppermute | solution.py:36
  46.6 12.5 %collective-permute-done.7 = bf16[64,4096]{1,0:T(8,128)(2,1)S(1)} collective-permute-done((bf16[64,4096]{1,0:T(8,128)(2,1)S(1)}, bf16[64,4096]{1,0:T(8,128)(2,1)S(1)}, u32[]{:S(2)}, u32[]{:S(2)}) %collective-permute-start.7) | collective-permute-done | bytes 524320 | tf_op jit(solution)/shard_map/ppermute | solution.py:36
  63.0 3.2 collective-permute-start.1
  66.2 9.2 %collective-permute-done = bf16[64,4096]{1,0:T(8,128)(2,1)S(1)} collective-permute-done((bf16[64,4096]{1,0:T(8,128)(2,1)S(1)}, bf16[64,4096]{1,0:T(8,128)(2,1)S(1)}, u32[]{:S(2)}, u32[]{:S(2)}) %collective-permute-start) | collective-permute-done | bytes 524320 | tf_op jit(solution)/shard_map/ppermute | solution.py:36
  75.6 3.3 collective-permute-start.3
  80.8 2.3 collective-permute-done.2
  84.7 2.0 copy-done.25
  87.9 6.0 %collective-permute-done.8 = bf16[512,4096]{1,0:T(8,128)(2,1)S(1)} collective-permute-done((bf16[512,4096]{1,0:T(8,128)(2,1)S(1)}, bf16[512,4096]{1,0:T(8,128)(2,1)S(1)}, u32[]{:S(2)}, u32[]{:S(2)}) %collective-permute-start.8) | collective-permute-done | bytes 4194336 | tf_op jit(solution)/shard_map/ppermute | solution.py:36
  93.9 3.0 slice_dynamic-update-slice_fusion.8
  100.1 2.6 collective-permute-start.10
  102.7 11.5 %collective-permute-done.10 = bf16[64,4096]{1,0:T(8,128)(2,1)S(1)} collective-permute-done((bf16[64,4096]{1,0:T(8,128)(2,1)S(1)}, bf16[64,4096]{1,0:T(8,128)(2,1)S(1)}, u32[]{:S(2)}, u32[]{:S(2)}) %collective-permute-start.10) | collective-permute-done | bytes 524320 | tf_op jit(solution)/shard_map/ppermute | solution.py:36
  115.0 2.0 copy.61
  117.0 17.8 %collective-permute-done.9 = bf16[256,4096]{1,0:T(8,128)(2,1)S(1)} collective-permute-done((bf16[256,4096]{1,0:T(8,128)(2,1)S(1)}, bf16[256,4096]{1,0:T(8,128)(2,1)S(1)}, u32[]{:S(2)}, u32[]{:S(2)}) %collective-permute-start.9) | collective-permute-done | bytes 2097184 | tf_op jit(solution)/shard_map/ppermute | solution.py:36
  134.8 1.7 constant_dynamic-update-slice_fusion.67
  137.0 13.8 %collective-permute-done.13 = bf16[64,4096]{1,0:T(8,128)(2,1)S(1)} collective-permute-done((bf16[64,4096]{1,0:T(8,128)(2,1)S(1)}, bf16[64,4096]{1,0:T(8,128)(2,1)S(1)}, u32[]{:S(2)}, u32[]{:S(2)}) %collective-permute-start.13) | collective-permute-done | bytes 524320 | tf_op jit(solution)/shard_map/ppermute | solution.py:36
  150.8 2.5 collective-permute-start.14
  153.4 2.2 collective-permute-start.12
  155.6 1.7 fusion.29
  160.2 2.6 multiply_convert_fusion.3
  162.8 2.4 fusion.21
  165.2 2.5 add_convert_fusion.1
  167.8 4.0 %constant_dynamic-update-slice_fusion.66 = (bf16[2048,4096]{1,0:T(8,128)(2,1)}, bf16[2048,4096]{1,0:T(8,128)(2,1)}, bf16[512,4096]{1,0:T(8,128)(2,1)}, bf16[256,4096]{1,0:T(8,128)(2,1)S(1)}) fusion(bf16[2048,4096]{1,0:T(8,128)(2,1)} %get-tuple-element.33, bf16[512,4096]{1,0:T(8,128)(2,1)S(1)} %collective-permute-done.11, ...), kind=kLoop, calls=%fused_computation.211 | loop fusion | bytes 12582912
  174.4 3.4 collective-permute-start.17
  177.8 4.0 %fusion.27 = f32[512,336]{0,1:T(8,128)S(1)} fusion(bf16[512,4096]{1,0:T(8,128)(2,1)} %get-tuple-element.18, bf16[1,336,4096]{2,1,0:T(8,128)(2,1)S(1)} %copy-done.3), kind=kOutput, calls=%fused_computation.39 | convolution fusion | flops 1409286144 | bytes 7634944 | tf_op jit(solution)/shard_map/dot_general | solution.py:56
  181.8 1.6 fusion.4
  184.0 2.5 multiply_convert_fusion.2
  186.6 2.4 fusion.19
  189.0 2.5 add_convert_fusion
  193.1 2.3 pad_maximum_fusion
  195.4 4.5 %collective-permute-done.16 = bf16[128,4096]{1,0:T(8,128)(2,1)} collective-permute-done((bf16[128,4096]{1,0:T(8,128)(2,1)}, bf16[128,4096]{1,0:T(8,128)(2,1)}, u32[]{:S(2)}, u32[]{:S(2)}) %collective-permute-start.16) | collective-permute-done | bytes 1048608 | tf_op jit(solution)/shard_map/ppermute | solution.py:36
  199.9 2.2 slice_dynamic-update-slice_fusion.12
  202.1 1.9 slice_dynamic-update-slice_fusion.15
  204.0 11.1 %collective-permute-done.18 = bf16[64,4096]{1,0:T(8,128)(2,1)S(1)} collective-permute-done((bf16[64,4096]{1,0:T(8,128)(2,1)S(1)}, bf16[64,4096]{1,0:T(8,128)(2,1)S(1)}, u32[]{:S(2)}, u32[]{:S(2)}) %collective-permute-start.18) | collective-permute-done | bytes 524320 | tf_op jit(solution)/shard_map/ppermute | solution.py:36
  215.9 2.0 copy.77
  218.0 1.8 constant_dynamic-update-slice_fusion.65
  219.7 2.6 collective-permute-start.24
  223.4 2.2 collective-permute-start.20
  229.0 1.9 collective-permute-start.31
  230.9 6.1 %constant_dynamic-update-slice_fusion.64 = (bf16[2048,4096]{1,0:T(8,128)(2,1)}, bf16[2048,4096]{1,0:T(8,128)(2,1)}, bf16[512,4096]{1,0:T(8,128)(2,1)}, bf16[256,4096]{1,0:T(8,128)(2,1)}) fusion(bf16[2048,4096]{1,0:T(8,128)(2,1)} %get-tuple-element.31, bf16[512,4096]{1,0:T(8,128)(2,1)} %collective-permute-done.19, bf16[2048,4096]{1,0:T(8,128)(2,1)} %get-tuple-element.87, ...), kind=kLoop, calls=%fused_computation.209 | loop fusion | bytes 12582912
  238.4 1.9 slice_dynamic-update-slice_fusion.10
  240.3 2.0 constant_dynamic-update-slice_fusion.41
  243.7 11.2 %collective-permute-done.31 = bf16[2,64,2048]{2,1,0:T(8,128)(2,1)S(1)} collective-permute-done((bf16[2,64,2048]{2,1,0:T(8,128)(2,1)S(1)}, bf16[2,64,2048]{2,1,0:T(8,128)(2,1)S(1)}, u32[]{:S(2)}, u32[]{:S(2)}) %collective-permute-start.31) | collective-permute-done | bytes 524320 | tf_op jit(solution)/shard_map/ppermute | solution.py:36
  256.6 10.9 %collective-permute-done.22 = bf16[64,4096]{1,0:T(8,128)(2,1)S(1)} collective-permute-done((bf16[64,4096]{1,0:T(8,128)(2,1)S(1)}, bf16[64,4096]{1,0:T(8,128)(2,1)S(1)}, u32[]{:S(2)}, u32[]{:S(2)}) %collective-permute-start.22) | collective-permute-done | bytes 524320 | tf_op jit(solution)/shard_map/ppermute | solution.py:36
  267.5 1.7 collective-permute-start.33
  270.6 2.4 constant_dynamic-update-slice_fusion.63
  274.3 6.7 %collective-permute-done.26 = bf16[256,2048]{1,0:T(8,128)(2,1)S(1)} collective-permute-done((bf16[256,2048]{1,0:T(8,128)(2,1)S(1)}, bf16[256,2048]{1,0:T(8,128)(2,1)S(1)}, u32[]{:S(2)}, u32[]{:S(2)}) %collective-permute-start.26) | collective-permute-done | bytes 1048608 | tf_op jit(solution)/shard_map/ppermute | solution.py:36
  281.5 2.0 collective-permute-start.28
  284.3 3.7 %collective-permute-done.27 = bf16[64,2048]{1,0:T(8,128)(2,1)S(1)} collective-permute-done((bf16[64,2048]{1,0:T(8,128)(2,1)S(1)}, bf16[64,2048]{1,0:T(8,128)(2,1)S(1)}, u32[]{:S(2)}, u32[]{:S(2)}) %collective-permute-start.27) | collective-permute-done | bytes 262176 | tf_op jit(solution)/shard_map/ppermute | solution.py:36
  288.1 6.6 %collective-permute-done.28 = bf16[64,2048]{1,0:T(8,128)(2,1)S(1)} collective-permute-done((bf16[64,2048]{1,0:T(8,128)(2,1)S(1)}, bf16[64,2048]{1,0:T(8,128)(2,1)S(1)}, u32[]{:S(2)}, u32[]{:S(2)}) %collective-permute-start.28) | collective-permute-done | bytes 262176 | tf_op jit(solution)/shard_map/ppermute | solution.py:36
  294.8 2.1 collective-permute-start.34
  299.1 1.8 fusion.25
  300.9 1.8 multiply_convert_fusion.1
  302.7 3.1 collective-permute-done.34
  305.9 2.1 fusion.3
  307.9 2.9 constant_dynamic-update-slice_fusion.61
  312.9 2.8 fusion.12
  315.8 1.9 multiply_convert_fusion
  317.7 13.3 %fusion.1 = bf16[1,336,4096]{2,1,0:T(8,128)(2,1)} fusion(bf16[2048,4096]{1,0:T(8,128)(2,1)} %get-tuple-element.9, bf16[512,336]{0,1:T(8,128)(2,1)S(1)} %get-tuple-element.46, bf16[512,336]{0,1:T(8,128)(2,1)S(1)} %get-tuple-element.43, bf16[512,336]{0,1:T(8,128)(2,1)S(1)} %copy-done.19, bf16[512,336]{0,1:T(8,128)(2,1)S(1)} %copy-done.17), kind=kOutput, calls=%fused_computation.7 | convolution fusion | flops 5644025856 | bytes 20905984 | tf_op jit(solution)/shard_map/dot_general | solution.py:62
  331.0 13.1 %fusion = bf16[1,336,4096]{2,1,0:T(8,128)(2,1)} fusion(bf16[2048,4096]{1,0:T(8,128)(2,1)} %get-tuple-element.9, bf16[512,336]{0,1:T(8,128)(2,1)S(1)} %get-tuple-element.45, bf16[512,336]{0,1:T(8,128)(2,1)S(1)} %get-tuple-element.42, bf16[512,336]{0,1:T(8,128)(2,1)S(1)} %copy-done.23, bf16[512,336]{0,1:T(8,128)(2,1)S(1)} %copy-done.21), kind=kOutput, calls=%fused_computation.6 | convolution fusion | flops 5644025856 | bytes 20905984 | tf_op jit(solution)/shard_map/dot_general | solution.py:62
  344.1 7.1 %fusion.2 = bf16[1,336,4096]{2,1,0:T(8,128)(2,1)} fusion(bf16[2048,4096]{1,0:T(8,128)(2,1)S(1)} %bitcast.116, bf16[512,336]{0,1:T(8,128)(2,1)S(1)} %get-tuple-element.44, bf16[512,336]{0,1:T(8,128)(2,1)S(1)} %get-tuple-element.41, bf16[512,336]{0,1:T(8,128)(2,1)S(1)} %copy-done.32, bf16[512,336]{0,1:T(8,128)(2,1)S(1)} %copy-done.31), kind=kOutput, calls=%fused_computation.8 | convolution fusion | flops 5644025856 | bytes 20905984 | tf_op jit(solution)/shard_map/dot_general | solution.py:62
  (166 shorter events, 43.7 us)
Async XLA Ops:
  0.6 159.6 %copy-start = (bf16[1,336,4096]{2,1,0:T(8,128)(2,1)S(1)}, bf16[1,336,4096]{2,1,0:T(8,128)(2,1)}, u32[]{:S(2)}) copy-start(bf16[1,336,4096]{2,1,0:T(8,128)(2,1)} %param.12) | copy-start | bytes 8257540
  4.6 13.7 %collective-permute-start.4 = (bf16[64,4096]{1,0:T(8,128)(2,1)S(1)}, bf16[64,4096]{1,0:T(8,128)(2,1)S(1)}, u32[]{:S(2)}, u32[]{:S(2)}) collective-permute-start(bf16[64,4096]{1,0:T(8,128)(2,1)S(1)} %get-tuple-element.109), channel_id=1, source_target_pairs={{0,2},{1,3},{4,6},{5,7},{8,10},{9,11},{12,14},{13,15},{2,0},{3,1},... | collective-permute-start | bytes 1572872 | tf_op jit(solution)/shard_map/ppermute | solution.py:36
  18.4 26.4 %collective-permute-start.5 = (bf16[128,4096]{1,0:T(8,128)(2,1)S(1)}, bf16[128,4096]{1,0:T(8,128)(2,1)S(1)}, u32[]{:S(2)}, u32[]{:S(2)}) collective-permute-start(bf16[128,4096]{1,0:T(8,128)(2,1)S(1)} %pad_maximum_fusion.2), channel_id=1, source_target_pairs={{0,4},{1,5},{4,8},{5,9},{8,12},{9,13},{12,0},{13,1},{2,6},{3,7},{6... | collective-permute-start | bytes 3145736 | tf_op jit(solution)/shard_map/ppermute | solution.py:36
  20.4 25.4 %collective-permute-start.6 = (bf16[128,4096]{1,0:T(8,128)(2,1)S(1)}, bf16[128,4096]{1,0:T(8,128)(2,1)S(1)}, u32[]{:S(2)}, u32[]{:S(2)}) collective-permute-start(bf16[128,4096]{1,0:T(8,128)(2,1)S(1)} %pad_maximum_fusion.2), channel_id=1, source_target_pairs={{0,12},{1,13},{4,0},{5,1},{8,4},{9,5},{12,8},{13,9},{2,14},{3,15},... | collective-permute-start | bytes 3145736 | tf_op jit(solution)/shard_map/ppermute | solution.py:36
  45.7 13.4 %collective-permute-start.7 = (bf16[64,4096]{1,0:T(8,128)(2,1)S(1)}, bf16[64,4096]{1,0:T(8,128)(2,1)S(1)}, u32[]{:S(2)}, u32[]{:S(2)}) collective-permute-start(bf16[64,4096]{1,0:T(8,128)(2,1)S(1)} %get-tuple-element.69), channel_id=1, source_target_pairs={{0,4},{1,5},{4,8},{5,9},{8,12},{9,13},{12,0},{13,1},{2,6},{3,7},{6... | collective-permute-start | bytes 1572872 | tf_op jit(solution)/shard_map/ppermute | solution.py:36
  63.0 12.4 %collective-permute-start = (bf16[64,4096]{1,0:T(8,128)(2,1)S(1)}, bf16[64,4096]{1,0:T(8,128)(2,1)S(1)}, u32[]{:S(2)}, u32[]{:S(2)}) collective-permute-start(bf16[64,4096]{1,0:T(8,128)(2,1)S(1)} %get-tuple-element.110), channel_id=1, source_target_pairs={{0,4},{1,5},{4,8},{5,9},{8,12},{9,13},{12,0},{13,1},{2,6},{3,7},{6... | collective-permute-start | bytes 1572872 | tf_op jit(solution)/shard_map/ppermute | solution.py:36
  63.0 12.5 %collective-permute-start.1 = (bf16[64,4096]{1,0:T(8,128)(2,1)S(1)}, bf16[64,4096]{1,0:T(8,128)(2,1)S(1)}, u32[]{:S(2)}, u32[]{:S(2)}) collective-permute-start(bf16[64,4096]{1,0:T(8,128)(2,1)S(1)} %get-tuple-element.110), channel_id=1, source_target_pairs={{0,12},{1,13},{4,0},{5,1},{8,4},{9,5},{12,8},{13,9},{2,14},{3,15},... | collective-permute-start | bytes 1572872 | tf_op jit(solution)/shard_map/ppermute | solution.py:36
  75.5 7.7 %collective-permute-start.2 = (bf16[32,4096]{1,0:T(8,128)(2,1)S(1)}, bf16[32,4096]{1,0:T(8,128)(2,1)S(1)}, u32[]{:S(2)}, u32[]{:S(2)}) collective-permute-start(bf16[32,4096]{1,0:T(8,128)(2,1)S(1)} %slice.184), channel_id=1, source_target_pairs={{0,4},{1,5},{4,8},{5,9},{8,12},{9,13},{12,0},{13,1},{2,6},{3,7},{6... | collective-permute-start | bytes 786440 | tf_op jit(solution)/shard_map/ppermute | solution.py:36
  75.6 8.3 %collective-permute-start.3 = (bf16[32,4096]{1,0:T(8,128)(2,1)S(1)}, bf16[32,4096]{1,0:T(8,128)(2,1)S(1)}, u32[]{:S(2)}, u32[]{:S(2)}) collective-permute-start(bf16[32,4096]{1,0:T(8,128)(2,1)S(1)} %slice.185), channel_id=1, source_target_pairs={{0,12},{1,13},{4,0},{5,1},{8,4},{9,5},{12,8},{13,9},{2,14},{3,15},... | collective-permute-start | bytes 786440 | tf_op jit(solution)/shard_map/ppermute | solution.py:36
  86.7 30.3 %copy-start.24 = (bf16[256,4096]{1,0:T(8,128)(2,1)}, bf16[256,4096]{1,0:T(8,128)(2,1)S(1)}, u32[]{:S(2)}) copy-start(bf16[256,4096]{1,0:T(8,128)(2,1)S(1)} %get-tuple-element.98) | copy-start | bytes 6291460
  86.7 7.2 %collective-permute-start.8 = (bf16[512,4096]{1,0:T(8,128)(2,1)S(1)}, bf16[512,4096]{1,0:T(8,128)(2,1)S(1)}, u32[]{:S(2)}, u32[]{:S(2)}) collective-permute-start(bf16[512,4096]{1,0:T(8,128)(2,1)S(1)} %get-tuple-element.100), channel_id=1, source_target_pairs={{0,1},{1,0},{4,5},{5,4},{8,9},{9,8},{12,13},{13,12},{2,3},{3,2},{6... | collective-permute-start | bytes 12582920 | tf_op jit(solution)/shard_map/ppermute | solution.py:36
  86.7 48.0 %collective-permute-start.9 = (bf16[256,4096]{1,0:T(8,128)(2,1)S(1)}, bf16[256,4096]{1,0:T(8,128)(2,1)S(1)}, u32[]{:S(2)}, u32[]{:S(2)}) collective-permute-start(bf16[256,4096]{1,0:T(8,128)(2,1)S(1)} %get-tuple-element.98), channel_id=1, source_target_pairs={{0,2},{1,3},{4,6},{5,7},{8,10},{9,11},{12,14},{13,15},{2,0},{3,1},... | collective-permute-start | bytes 6291464 | tf_op jit(solution)/shard_map/ppermute | solution.py:36
  96.9 20.1 %copy-start.7 = (bf16[512,4096]{1,0:T(8,128)(2,1)}, bf16[512,4096]{1,0:T(8,128)(2,1)S(1)}, u32[]{:S(2)}) copy-start(bf16[512,4096]{1,0:T(8,128)(2,1)S(1)} %get-tuple-element.22) | copy-start | bytes 12582916
  100.1 14.0 %collective-permute-start.10 = (bf16[64,4096]{1,0:T(8,128)(2,1)S(1)}, bf16[64,4096]{1,0:T(8,128)(2,1)S(1)}, u32[]{:S(2)}, u32[]{:S(2)}) collective-permute-start(bf16[64,4096]{1,0:T(8,128)(2,1)S(1)} %get-tuple-element.65), channel_id=1, source_target_pairs={{0,12},{1,13},{4,0},{5,1},{8,4},{9,5},{12,8},{13,9},{2,14},{3,15},... | collective-permute-start | bytes 1572872 | tf_op jit(solution)/shard_map/ppermute | solution.py:36
  117.0 38.5 %copy-start.3 = (bf16[1,336,4096]{2,1,0:T(8,128)(2,1)S(1)}, bf16[1,336,4096]{2,1,0:T(8,128)(2,1)}, u32[]{:S(2)}) copy-start(bf16[1,336,4096]{2,1,0:T(8,128)(2,1)} %param.11) | copy-start | bytes 8257540
  134.8 22.5 %copy-start.4 = (bf16[256,4096]{1,0:T(8,128)(2,1)}, bf16[256,4096]{1,0:T(8,128)(2,1)S(1)}, u32[]{:S(2)}) copy-start(bf16[256,4096]{1,0:T(8,128)(2,1)S(1)} %collective-permute-done.9) | copy-start | bytes 6291460
  134.8 20.8 %copy-start.8 = (bf16[512,4096]{1,0:T(8,128)(2,1)S(1)}, bf16[512,4096]{1,0:T(8,128)(2,1)}, u32[]{:S(2)}) copy-start(bf16[512,4096]{1,0:T(8,128)(2,1)} %copy-done.7) | copy-start | bytes 12582916
  136.4 31.3 %collective-permute-start.11 = (bf16[512,4096]{1,0:T(8,128)(2,1)S(1)}, bf16[512,4096]{1,0:T(8,128)(2,1)S(1)}, u32[]{:S(2)}, u32[]{:S(2)}) collective-permute-start(bf16[512,4096]{1,0:T(8,128)(2,1)S(1)} %get-tuple-element.34), channel_id=1, source_target_pairs={{0,1},{1,0},{4,5},{5,4},{8,9},{9,8},{12,13},{13,12},{2,3},{3,2},{6... | collective-permute-start | bytes 12582920 | tf_op jit(solution)/shard_map/ppermute | solution.py:36
  136.4 14.3 %collective-permute-start.13 = (bf16[64,4096]{1,0:T(8,128)(2,1)S(1)}, bf16[64,4096]{1,0:T(8,128)(2,1)S(1)}, u32[]{:S(2)}, u32[]{:S(2)}) collective-permute-start(bf16[64,4096]{1,0:T(8,128)(2,1)S(1)} %get-tuple-element.109), channel_id=1, source_target_pairs={{0,66},{1,67},{4,70},{5,71},{8,74},{9,75},{12,78},{13,79},{2,64},{... | collective-permute-start | bytes 1572872 | tf_op jit(solution)/shard_map/ppermute | solution.py:36
  150.8 22.1 %collective-permute-start.14 = (bf16[32,4096]{1,0:T(8,128)(2,1)S(1)}, bf16[32,4096]{1,0:T(8,128)(2,1)S(1)}, u32[]{:S(2)}, u32[]{:S(2)}) collective-permute-start(bf16[32,4096]{1,0:T(8,128)(2,1)S(1)} %slice.194), channel_id=1, source_target_pairs={{0,2},{1,3},{4,6},{5,7},{8,10},{9,11},{12,14},{13,15},{2,0},{3,1},... | collective-permute-start | bytes 786440 | tf_op jit(solution)/shard_map/ppermute | solution.py:36
  153.3 20.4 %collective-permute-start.15 = (bf16[32,4096]{1,0:T(8,128)(2,1)S(1)}, bf16[32,4096]{1,0:T(8,128)(2,1)S(1)}, u32[]{:S(2)}, u32[]{:S(2)}) collective-permute-start(bf16[32,4096]{1,0:T(8,128)(2,1)S(1)} %slice.195), channel_id=1, source_target_pairs={{0,66},{1,67},{4,70},{5,71},{8,74},{9,75},{12,78},{13,79},{2,64},{... | collective-permute-start | bytes 786440 | tf_op jit(solution)/shard_map/ppermute | solution.py:36
  153.4 64.6 %collective-permute-start.12 = (bf16[256,4096]{1,0:T(8,128)(2,1)}, bf16[256,4096]{1,0:T(8,128)(2,1)S(1)}, u32[]{:S(2)}, u32[]{:S(2)}) collective-permute-start(bf16[256,4096]{1,0:T(8,128)(2,1)} %copy-done.24), channel_id=1, source_target_pairs={{0,66},{1,67},{4,70},{5,71},{8,74},{9,75},{12,78},{13,79},{2,64},{... | collective-permute-start | bytes 6291464 | tf_op jit(solution)/shard_map/ppermute | solution.py:36
  155.5 2.2 copy-start.26
  155.5 3.1 copy-start.27
  162.8 2.4 copy-start.20
  162.8 2.4 copy-start.16
  167.7 4.0 %copy-start.1 = (bf16[512,4096]{1,0:T(8,128)(2,1)}, bf16[512,4096]{1,0:T(8,128)(2,1)S(1)}, u32[]{:S(2)}) copy-start(bf16[512,4096]{1,0:T(8,128)(2,1)S(1)} %add_convert_fusion.1) | copy-start | bytes 12582916
  174.4 25.5 %collective-permute-start.16 = (bf16[128,4096]{1,0:T(8,128)(2,1)}, bf16[128,4096]{1,0:T(8,128)(2,1)}, u32[]{:S(2)}, u32[]{:S(2)}) collective-permute-start(bf16[128,4096]{1,0:T(8,128)(2,1)} %get-tuple-element.106), channel_id=1, source_target_pairs={{0,4},{1,5},{4,8},{5,9},{8,12},{9,13},{12,0},{13,1},{2,6},{3,7},{6... | collective-permute-start | bytes 3145736 | tf_op jit(solution)/shard_map/ppermute | solution.py:36
  174.4 27.7 %collective-permute-start.17 = (bf16[128,4096]{1,0:T(8,128)(2,1)}, bf16[128,4096]{1,0:T(8,128)(2,1)}, u32[]{:S(2)}, u32[]{:S(2)}) collective-permute-start(bf16[128,4096]{1,0:T(8,128)(2,1)} %get-tuple-element.106), channel_id=1, source_target_pairs={{0,12},{1,13},{4,0},{5,1},{8,4},{9,5},{12,8},{13,9},{2,14},{3,15},... | collective-permute-start | bytes 3145736 | tf_op jit(solution)/shard_map/ppermute | solution.py:36
  177.8 4.0 %copy-start.5 = (bf16[256,4096]{1,0:T(8,128)(2,1)S(1)}, bf16[256,4096]{1,0:T(8,128)(2,1)}, u32[]{:S(2)}) copy-start(bf16[256,4096]{1,0:T(8,128)(2,1)} %copy-done.4) | copy-start | bytes 6291460
  177.8 4.0 %copy-start.28 = (bf16[1,336,4096]{2,1,0:T(8,128)(2,1)S(1)}, bf16[1,336,4096]{2,1,0:T(8,128)(2,1)}, u32[]{:S(2)}) copy-start(bf16[1,336,4096]{2,1,0:T(8,128)(2,1)} %param.13) | copy-start | bytes 8257540
  181.8 2.2 copy-start.10
  186.6 2.4 copy-start.22
  186.6 2.4 copy-start.18
  195.4 31.2 %collective-permute-start.25 = (bf16[512,4096]{1,0:T(8,128)(2,1)}, bf16[512,4096]{1,0:T(8,128)(2,1)S(1)}, u32[]{:S(2)}, u32[]{:S(2)}) collective-permute-start(bf16[512,4096]{1,0:T(8,128)(2,1)} %pad_maximum_fusion), channel_id=1, source_target_pairs={{0,1},{1,0},{4,5},{5,4},{8,9},{9,8},{12,13},{13,12},{2,3},{3,2},{6... | collective-permute-start | bytes 12582920 | tf_op jit(solution)/shard_map/ppermute | solution.py:36
  202.1 13.0 %collective-permute-start.18 = (bf16[64,4096]{1,0:T(8,128)(2,1)S(1)}, bf16[64,4096]{1,0:T(8,128)(2,1)S(1)}, u32[]{:S(2)}, u32[]{:S(2)}) collective-permute-start(bf16[64,4096]{1,0:T(8,128)(2,1)S(1)} %get-tuple-element.60), channel_id=1, source_target_pairs={{0,4},{1,5},{4,8},{5,9},{8,12},{9,13},{12,0},{13,1},{2,6},{3,7},{6... | collective-permute-start | bytes 1572872 | tf_op jit(solution)/shard_map/ppermute | solution.py:36
  218.0 7.6 %copy-start.6 = (bf16[256,4096]{1,0:T(8,128)(2,1)S(1)}, bf16[256,4096]{1,0:T(8,128)(2,1)}, u32[]{:S(2)}) copy-start(bf16[256,4096]{1,0:T(8,128)(2,1)} %copy-done.4) | copy-start | bytes 6291460
  218.0 8.6 %copy-start.2 = (bf16[512,4096]{1,0:T(8,128)(2,1)S(1)}, bf16[512,4096]{1,0:T(8,128)(2,1)}, u32[]{:S(2)}) copy-start(bf16[512,4096]{1,0:T(8,128)(2,1)} %copy-done.1) | copy-start | bytes 12582916
  219.7 11.1 %collective-permute-start.19 = (bf16[512,4096]{1,0:T(8,128)(2,1)S(1)}, bf16[512,4096]{1,0:T(8,128)(2,1)}, u32[]{:S(2)}, u32[]{:S(2)}) collective-permute-start(bf16[512,4096]{1,0:T(8,128)(2,1)S(1)} %get-tuple-element.32), channel_id=1, source_target_pairs={{0,1},{1,0},{4,5},{5,4},{8,9},{9,8},{12,13},{13,12},{2,3},{3,2},{6... | collective-permute-start | bytes 12582920 | tf_op jit(solution)/shard_map/ppermute | solution.py:36
  219.7 83.0 %collective-permute-start.24 = (s32[256]{0:T(256)S(1)}, s32[256]{0:T(256)S(1)}, u32[]{:S(2)}, u32[]{:S(2)}) collective-permute-start(s32[256]{0:T(256)S(1)} %broadcast_select_fusion), channel_id=1, source_target_pairs={{16,0},{32,16},{48,32},{17,1},{33,17},{49,33},{18,2},{34,18},{50,3... | collective-permute-start | bytes 3080 | tf_op jit(solution)/shard_map/ppermute | solution.py:95
  223.4 47.2 %collective-permute-start.20 = (bf16[128,4096]{1,0:T(8,128)(2,1)}, bf16[128,4096]{1,0:T(8,128)(2,1)}, u32[]{:S(2)}, u32[]{:S(2)}) collective-permute-start(bf16[128,4096]{1,0:T(8,128)(2,1)} %slice.200), channel_id=1, source_target_pairs={{0,2},{1,3},{4,6},{5,7},{8,10},{9,11},{12,14},{13,15},{2,0},{3,1},... | collective-permute-start | bytes 3145736 | tf_op jit(solution)/shard_map/ppermute | solution.py:36
  228.8 14.9 %collective-permute-start.30 = (bf16[2,64,2048]{2,1,0:T(8,128)(2,1)S(1)}, bf16[2,64,2048]{2,1,0:T(8,128)(2,1)S(1)}, u32[]{:S(2)}, u32[]{:S(2)}) collective-permute-start(bf16[2,64,2048]{2,1,0:T(8,128)(2,1)S(1)} %get-tuple-element.28), channel_id=1, source_target_pairs={{0,12},{1,13},{4,0},{5,1},{8,4},{9,5},{12,8},{13,9},{2,14},{3,15},... | collective-permute-start | bytes 1572872 | tf_op jit(solution)/shard_map/ppermute | solution.py:36
  229.0 25.9 %collective-permute-start.31 = (bf16[2,64,2048]{2,1,0:T(8,128)(2,1)S(1)}, bf16[2,64,2048]{2,1,0:T(8,128)(2,1)S(1)}, u32[]{:S(2)}, u32[]{:S(2)}) collective-permute-start(bf16[2,64,2048]{2,1,0:T(8,128)(2,1)S(1)} %get-tuple-element.29), channel_id=1, source_target_pairs={{0,4},{1,5},{4,8},{5,9},{8,12},{9,13},{12,0},{13,1},{2,6},{3,7},{6... | collective-permute-start | bytes 1572872 | tf_op jit(solution)/shard_map/ppermute | solution.py:36
  230.9 24.3 %collective-permute-start.32 = (bf16[2,64,2048]{2,1,0:T(8,128)(2,1)S(1)}, bf16[2,64,2048]{2,1,0:T(8,128)(2,1)S(1)}, u32[]{:S(2)}, u32[]{:S(2)}) collective-permute-start(bf16[2,64,2048]{2,1,0:T(8,128)(2,1)S(1)} %get-tuple-element.30), channel_id=1, source_target_pairs={{0,8},{1,9},{4,12},{5,13},{8,0},{9,1},{12,4},{13,5},{2,10},{3,11},... | collective-permute-start | bytes 1572872 | tf_op jit(solution)/shard_map/ppermute | solution.py:36
  237.0 6.7 %copy-start.15 = (bf16[128,4096]{1,0:T(8,128)(2,1)S(1)}, bf16[128,4096]{1,0:T(8,128)(2,1)}, u32[]{:S(2)}) copy-start(bf16[128,4096]{1,0:T(8,128)(2,1)} %slice.201) | copy-start | bytes 3145732
  243.7 29.3 %collective-permute-start.21 = (bf16[128,4096]{1,0:T(8,128)(2,1)S(1)}, bf16[128,4096]{1,0:T(8,128)(2,1)S(1)}, u32[]{:S(2)}, u32[]{:S(2)}) collective-permute-start(bf16[128,4096]{1,0:T(8,128)(2,1)S(1)} %copy-done.15), channel_id=1, source_target_pairs={{0,66},{1,67},{4,70},{5,71},{8,74},{9,75},{12,78},{13,79},{2,64},{... | collective-permute-start | bytes 3145736 | tf_op jit(solution)/shard_map/ppermute | solution.py:36
  254.9 26.1 %collective-permute-start.26 = (bf16[256,2048]{1,0:T(8,128)(2,1)S(1)}, bf16[256,2048]{1,0:T(8,128)(2,1)S(1)}, u32[]{:S(2)}, u32[]{:S(2)}) collective-permute-start(bf16[256,2048]{1,0:T(8,128)(2,1)S(1)} %get-tuple-element.26), channel_id=1, source_target_pairs={{0,2},{1,3},{4,6},{5,7},{8,10},{9,11},{12,14},{13,15},{2,0},{3,1},... | collective-permute-start | bytes 3145736 | tf_op jit(solution)/shard_map/ppermute | solution.py:36
  255.2 12.3 %collective-permute-start.22 = (bf16[64,4096]{1,0:T(8,128)(2,1)S(1)}, bf16[64,4096]{1,0:T(8,128)(2,1)S(1)}, u32[]{:S(2)}, u32[]{:S(2)}) collective-permute-start(bf16[64,4096]{1,0:T(8,128)(2,1)S(1)} %get-tuple-element.56), channel_id=1, source_target_pairs={{0,12},{1,13},{4,0},{5,1},{8,4},{9,5},{12,8},{13,9},{2,14},{3,15},... | collective-permute-start | bytes 1572872 | tf_op jit(solution)/shard_map/ppermute | solution.py:36
  267.5 16.8 %collective-permute-start.33 = (bf16[64,2048]{1,0:T(8,128)(2,1)S(1)}, bf16[64,2048]{1,0:T(8,128)(2,1)S(1)}, u32[]{:S(2)}, u32[]{:S(2)}) collective-permute-start(bf16[64,2048]{1,0:T(8,128)(2,1)S(1)} %fusion.80), channel_id=1, source_target_pairs={{0,2},{1,3},{4,6},{5,7},{8,10},{9,11},{12,14},{13,15},{2,0},{3,1},... | collective-permute-start | bytes 786440 | tf_op jit(solution)/shard_map/ppermute | solution.py:36
  274.2 22.7 %copy-start.12 = (bf16[256,4096]{1,0:T(8,128)(2,1)S(1)}, bf16[256,4096]{1,0:T(8,128)(2,1)}, u32[]{:S(2)}) copy-start(bf16[256,4096]{1,0:T(8,128)(2,1)} %get-tuple-element.15) | copy-start | bytes 6291460
  274.2 22.7 %copy-start.29 = (bf16[1,336,4096]{2,1,0:T(8,128)(2,1)S(1)}, bf16[1,336,4096]{2,1,0:T(8,128)(2,1)}, u32[]{:S(2)}) copy-start(bf16[1,336,4096]{2,1,0:T(8,128)(2,1)} %param.13) | copy-start | bytes 8257540
  274.2 33.7 %collective-permute-start.23 = (bf16[512,4096]{1,0:T(8,128)(2,1)S(1)}, bf16[512,4096]{1,0:T(8,128)(2,1)S(1)}, u32[]{:S(2)}, u32[]{:S(2)}) collective-permute-start(bf16[512,4096]{1,0:T(8,128)(2,1)S(1)} %get-tuple-element.51), channel_id=1, source_target_pairs={{0,1},{1,0},{4,5},{5,4},{8,9},{9,8},{12,13},{13,12},{2,3},{3,2},{6... | collective-permute-start | bytes 12582920 | tf_op jit(solution)/shard_map/ppermute | solution.py:36
  281.5 6.6 %collective-permute-start.27 = (bf16[64,2048]{1,0:T(8,128)(2,1)S(1)}, bf16[64,2048]{1,0:T(8,128)(2,1)S(1)}, u32[]{:S(2)}, u32[]{:S(2)}) collective-permute-start(bf16[64,2048]{1,0:T(8,128)(2,1)S(1)} %get-tuple-element.47), channel_id=1, source_target_pairs={{0,12},{1,13},{4,0},{5,1},{8,4},{9,5},{12,8},{13,9},{2,14},{3,15},... | collective-permute-start | bytes 786440 | tf_op jit(solution)/shard_map/ppermute | solution.py:36
  281.5 13.1 %collective-permute-start.28 = (bf16[64,2048]{1,0:T(8,128)(2,1)S(1)}, bf16[64,2048]{1,0:T(8,128)(2,1)S(1)}, u32[]{:S(2)}, u32[]{:S(2)}) collective-permute-start(bf16[64,2048]{1,0:T(8,128)(2,1)S(1)} %get-tuple-element.49), channel_id=1, source_target_pairs={{0,4},{1,5},{4,8},{5,9},{8,12},{9,13},{12,0},{13,1},{2,6},{3,7},{6... | collective-permute-start | bytes 786440 | tf_op jit(solution)/shard_map/ppermute | solution.py:36
  284.3 10.3 %collective-permute-start.29 = (bf16[64,2048]{1,0:T(8,128)(2,1)S(1)}, bf16[64,2048]{1,0:T(8,128)(2,1)S(1)}, u32[]{:S(2)}, u32[]{:S(2)}) collective-permute-start(bf16[64,2048]{1,0:T(8,128)(2,1)S(1)} %get-tuple-element.48), channel_id=1, source_target_pairs={{0,8},{1,9},{4,12},{5,13},{8,0},{9,1},{12,4},{13,5},{2,10},{3,11},... | collective-permute-start | bytes 786440 | tf_op jit(solution)/shard_map/ppermute | solution.py:36
  294.8 11.1 %collective-permute-start.34 = (bf16[64,4096]{1,0:T(8,128)(2,1)S(1)}, bf16[64,4096]{1,0:T(8,128)(2,1)S(1)}, u32[]{:S(2)}, u32[]{:S(2)}) collective-permute-start(bf16[64,4096]{1,0:T(8,128)(2,1)S(1)} %pad_maximum_fusion.3), channel_id=1, source_target_pairs={{16,0},{32,16},{48,32},{17,1},{33,17},{49,33},{18,2},{34,18},{50,3... | collective-permute-start | bytes 1572872 | tf_op jit(solution)/shard_map/ppermute | solution.py:152
  317.7 13.3 %copy-start.21 = (bf16[512,336]{0,1:T(8,128)(2,1)S(1)}, bf16[512,336]{0,1:T(8,128)(2,1)}, u32[]{:S(2)}) copy-start(bf16[512,336]{0,1:T(8,128)(2,1)} %copy-done.20) | copy-start | bytes 1032196
  317.7 13.3 %copy-start.23 = (bf16[512,336]{0,1:T(8,128)(2,1)S(1)}, bf16[512,336]{0,1:T(8,128)(2,1)}, u32[]{:S(2)}) copy-start(bf16[512,336]{0,1:T(8,128)(2,1)} %copy-done.22) | copy-start | bytes 1032196
  317.7 26.4 %slice-start.1 = ((s8[16777216]{0:T(1024)(128)(4,1)}), s8[4194304]{0:T(1024)(128)(4,1)S(1)}, s32[]{:S(2)}) async-start(s8[16777216]{0:T(1024)(128)(4,1)} %bitcast.115), calls=%async_computation.1 | async-start | bytes 8388608
  317.7 26.4 %slice-start.2 = ((s8[16777216]{0:T(1024)(128)(4,1)}), s8[4194304]{0:T(1024)(128)(4,1)S(1)}, s32[]{:S(2)}) async-start(s8[16777216]{0:T(1024)(128)(4,1)} %bitcast.115), calls=%async_computation.2 | async-start | bytes 8388608
  331.0 13.1 %slice-start.3 = ((s8[16777216]{0:T(1024)(128)(4,1)}), s8[4194304]{0:T(1024)(128)(4,1)S(1)}, s32[]{:S(2)}) async-start(s8[16777216]{0:T(1024)(128)(4,1)} %bitcast.115), calls=%async_computation.3 | async-start | bytes 8388608
  331.0 13.1 %slice-start.4 = ((s8[16777216]{0:T(1024)(128)(4,1)}), s8[4194304]{0:T(1024)(128)(4,1)S(1)}, s32[]{:S(2)}) async-start(s8[16777216]{0:T(1024)(128)(4,1)} %bitcast.115), calls=%async_computation.4 | async-start | bytes 8388608
  331.0 13.1 %copy-start.31 = (bf16[512,336]{0,1:T(8,128)(2,1)S(1)}, bf16[512,336]{0,1:T(8,128)(2,1)}, u32[]{:S(2)}) copy-start(bf16[512,336]{0,1:T(8,128)(2,1)} %get-tuple-element.35) | copy-start | bytes 1032196
  331.0 13.1 %copy-start.32 = (bf16[512,336]{0,1:T(8,128)(2,1)S(1)}, bf16[512,336]{0,1:T(8,128)(2,1)}, u32[]{:S(2)}) copy-start(bf16[512,336]{0,1:T(8,128)(2,1)} %get-tuple-element.38) | copy-start | bytes 1032196
  (9 other events, 16.3 us)
